TPU v7x, 128 devices: a whole 4x4x4 slice. The times are simulated.
128 devices in a mesh: row: 8 (over y, core), col: 16 (over x, z).
Axes of the slice: x: 4, y: 4, z: 4, core: 2. Of those that a mesh axis runs over, the one named last changes fastest.
Arguments:
- features: bfloat16 [262144, 128], P(('row', 'col')), may hold values from -6 to 6
- new_index: int32 [262144], P(('row', 'col')), may hold values from 0 to 262143, as said below
- tile_values: bfloat16 [8, 16, 640, 128, 128], P('row', 'col'), may hold values from -0.125 to 0.125
- tile_index: int32 [8, 16, 2, 640], P('row', 'col'), may hold values from 0 to 255, as said below
- tile_count: int32 [8, 16], P('row', 'col'), may hold values from 80 to 640, as said below
- weight: bfloat16 [128, 256], replicated, may hold values from -0.5 to 0.5
- bias: float32 [256], replicated, may hold values from -3 to 3
Outputs:
- hidden: bfloat16 [262144, 256], P(('row', 'col'))
Inputs may be any that keep to these rules, and one draw needn't show every extreme that they name: A permutation. The new owner of a vertex is k = new_index // 2048; owner k is the device at grid row k mod the number of grid rows and grid column k div that number. From one device to one new owner at most 32 vertices move, and exactly 32 do for some pair in every draw. `tile_index`: entry 0 of a slot is a row tile below 256, entry 1 a column tile below 128; the slots of one grid block name distinct tiles. `tile_count`: some grid block holds 640 nonzero tiles in every draw.
All inputs are finite; a program needn't handle non-finite values.
Results may differ from a plain program's by a relative error of at most 0.017.
Values may be sent and summed in bfloat16 or wider, within the bound.
No kernel may reach another device: no remote copies, remote signals or barrier semaphores. Data moves between devices by JAX's collectives and lax.ppermute only.
A program may use at most 128 MiB of HBM per device.

v0:
```python
import jax
import jax.numpy as jnp
from jax import lax
from jax.sharding import PartitionSpec as P

GROUP = 64


def body(features, new_index, tile_values, tile_index, tile_count, weight, bias):
    grid_rows = lax.axis_size("row")
    grid_cols = lax.axis_size("col")
    device_total = grid_rows * grid_cols
    local_rows = features.shape[0]
    feature_width = features.shape[1]
    capacity = 2 * local_rows // device_total
    new_owner = new_index // local_rows
    new_slot = new_index % local_rows
    target_peer = new_owner % grid_rows * grid_cols + new_owner // grid_rows
    peer_hits = (target_peer[:, None] == jnp.arange(device_total, dtype=jnp.int32)[None, :]).astype(
        jnp.int32
    )
    peer_rank = jnp.sum((jnp.cumsum(peer_hits, axis=0) - peer_hits) * peer_hits, axis=1)
    outgoing = (
        jnp.zeros((device_total, capacity, feature_width), jnp.bfloat16)
        .at[target_peer, peer_rank]
        .set(features)
    )
    slots_out = (
        jnp.full((device_total, capacity), local_rows, jnp.int32)
        .at[target_peer, peer_rank]
        .set(new_slot)
    )
    rows_in, slots_in = (
        lax.all_to_all(outgoing, ("row", "col"), split_axis=0, concat_axis=0, tiled=True),
        lax.all_to_all(slots_out, ("row", "col"), split_axis=0, concat_axis=0, tiled=True),
    )
    moved_rows = (
        jnp.zeros((local_rows, feature_width), jnp.bfloat16)
        .at[slots_in.reshape(-1)]
        .set(rows_in.reshape(-1, feature_width), mode="drop")
    )
    column_block = lax.all_gather(moved_rows, "row", axis=0, tiled=True)
    tile_set = tile_values[0, 0]
    tile_coords = tile_index[0, 0]
    tile_total = tile_count[0, 0]
    tile_edge = tile_set.shape[1]
    col_tiles = column_block.shape[0] // tile_edge
    row_tiles = local_rows * grid_cols // tile_edge
    input_tiles = column_block.reshape(col_tiles, tile_edge, feature_width)

    def add_tiles(step_index, totals):
        first_tile = step_index * GROUP
        part_tiles = lax.dynamic_slice_in_dim(tile_set, first_tile, GROUP, 0)
        part_rows = lax.dynamic_slice_in_dim(tile_coords[0], first_tile, GROUP, 0)
        part_cols = lax.dynamic_slice_in_dim(tile_coords[1], first_tile, GROUP, 0)
        inputs = input_tiles[part_cols]
        products = jnp.einsum(
            "tab,tbf->taf", part_tiles, inputs, preferred_element_type=jnp.float32
        )
        live_mask = first_tile + jnp.arange(GROUP, dtype=jnp.int32) < tile_total
        products = jnp.where(live_mask[:, None, None], products, jnp.zeros_like(products))
        return totals.at[part_rows].add(products)

    trips = (tile_total + GROUP - 1) // GROUP
    totals = lax.fori_loop(
        0, trips, add_tiles, jnp.zeros((row_tiles, tile_edge, feature_width), jnp.float32)
    )
    partial_rows = totals.reshape(row_tiles * tile_edge, feature_width)
    row_totals = lax.psum_scatter(
        partial_rows.astype(jnp.bfloat16), "col", scatter_dimension=0, tiled=True
    )
    hidden = jnp.dot(row_totals, weight, preferred_element_type=jnp.float32) + bias
    return jnp.maximum(hidden, 0.0).astype(jnp.bfloat16)


def solution(mesh):
    in_specs = (
        P(("row", "col"), None),
        P(("row", "col")),
        P("row", "col", None, None, None),
        P("row", "col", None, None),
        P("row", "col"),
        P(),
        P(),
    )
    out_specs = P(("row", "col"), None)
    return jax.shard_map(body, mesh=mesh, in_specs=in_specs, out_specs=out_specs, check_vma=False)
```

profile of v0, /device:TPU:0, one launch (start us, length us, event | category | flops | bytes accessed | tf_op | source)
XLA Modules:
  0.0 434.0 jit_solution(357774305717248672)
XLA Ops:
  6.5 0.0 copy-start
  6.5 0.0 copy-start.4
  6.5 0.0 copy-start.2
  6.5 0.0 copy-start.3
  6.5 0.7 compare_select_fusion.4
  7.3 0.1 copy.13
  7.4 0.3 fusion.10
  7.8 0.1 broadcast_add_fusion
  7.9 0.3 copy.14
  8.2 0.6 fusion.9
  8.9 0.0 copy-done.4
  8.9 0.1 and_reduce_fusion
  9.0 0.0 copy-done.2
  9.0 0.0 copy-done.3
  9.0 0.1 multiply_reduce_fusion
  9.1 8.1 %scatter_custom_fusion.2 = s32[4096]{0:T(1024)S(1)} fusion(s32[2048]{0:T(1024)S(1)} %get-tuple-element.68, s32[2048]{0:T(1024)S(1)} %get-tuple-element.66, s32[]{:T(128)} %constant.93.clone.1), kind=kCustom, calls=%fused_computation.54 | custom fusion | bytes 16388
  17.2 0.7 copy.15
  17.9 11.1 %all-to-all-start = ((s32[128,1,32]{2,1,0:T(1,128)}), s32[128,1,32]{2,1,0:T(1,128)S(1)}, u32[]{:S(2)}, u32[]{:S(2)}) async-start(s32[128,1,32]{2,1,0:T(1,128)} %copy.15), calls=%async_computation | async-start | bytes 131072 | tf_op jit(solution)/shard_map/all_to_all | solution.py:35
  29.1 7.1 %scatter_custom_fusion.3 = bf16[4096,128]{1,0:T(8,128)(2,1)} fusion(s32[2048]{0:T(1024)S(1)} %get-tuple-element.67, bf16[2048,128]{1,0:T(8,128)(2,1)} %param.9, bf16[]{:T(256)} %constant.92.clone.1), kind=kCustom, calls=%fused_computation.28 | custom fusion | bytes 1049088
  36.2 2.3 all-to-all-done
  38.5 7.4 %all-to-all-start.1 = ((bf16[128,32,128]{2,1,0:T(8,128)(2,1)}), bf16[128,32,128]{2,1,0:T(8,128)(2,1)S(1)}, u32[]{:S(2)}, u32[]{:S(2)}) async-start(bf16[128,32,128]{2,1,0:T(8,128)(2,1)} %bitcast.17), calls=%async_computation.1 | async-start | bytes 2097152 | tf_op jit(solution)/shard_map/all_to_all | solution.py:34
  46.0 0.0 all-gather.2.cloned.1.call-start
  46.0 0.6 broadcast.174
  46.6 0.8 reduce.10
  47.5 0.1 reshape.136
  47.6 17.4 %all-to-all-done.1 = bf16[128,32,128]{2,1,0:T(8,128)(2,1)S(1)} async-done(((bf16[128,32,128]{2,1,0:T(8,128)(2,1)}), bf16[128,32,128]{2,1,0:T(8,128)(2,1)S(1)}, u32[]{:S(2)}, u32[]{:S(2)}) %all-to-all-start.1) | async-done | bytes 1048608 | tf_op jit(solution)/shard_map/all_to_all | solution.py:34
  65.0 11.6 %scatter_custom_fusion.1 = bf16[2048,128]{1,0:T(8,128)(2,1)} fusion(s32[4096]{0:T(1024)S(1)} %bitcast.65, bf16[4096,128]{1,0:T(8,128)(2,1)S(1)} %bitcast.58, bf16[]{:T(256)} %constant.92.clone.1), kind=kCustom, calls=%fused_computation.32 | custom fusion | bytes 524290 | tf_op jit(solution)/shard_map/scatter | solution.py:40
  76.6 0.0 all-gather.2.cloned.1.call-update
  76.6 0.0 reduce-scatter.2.cloned.1.call-start
  77.3 27.0 %all-gather.2.cloned.1.call-done = bf16[16384,128]{1,0:T(8,128)(2,1)} async-done(((bf16[2048,128]{1,0:T(8,128)(2,1)}), bf16[16384,128]{1,0:T(8,128)(2,1)}) %all-gather.2.cloned.1.call-update) | async-done | bytes 4194320 | tf_op jit(solution)/shard_map/all_gather | solution.py:42
  104.4 0.0 copy-start.1
  104.4 7.8 %broadcast_in_dim.15 = f32[256,128,128]{2,1,0:T(8,128)} broadcast(f32[]{:T(128)} %constant.87.clone.1), dimensions={} | broadcast | bytes 16777220 | tf_op jit(solution)/shard_map/broadcast_in_dim | solution.py:66
  112.2 0.0 copy-done.1
  112.2 43.7 %while.10 = (s32[]{:T(128)}, f32[256,128,128]{2,1,0:T(8,128)}, s32[]{:T(128)}, s32[2,640]{1,0:T(2,128)S(1)}, s32[]{:T(128)}, /*index=5*/bf16[640,128,128]{2,1,0:...) while((s32[]{:T(128)}, f32[256,128,128]{2,1,0:T(8,128)}, ...), condition=%wide.region_8.9_spmd, body=%wide.region_6.8_spmd.sunk | while | flops 270534144 | bytes 25182252 | solution.py:65
  112.2 0.7 add_compare_fusion.2
  112.9 0.1 fusion.39
  113.0 3.1 gather_fusion
  116.1 4.3 convolution_select_fusion.2
  120.4 13.7 %scatter_fusion = f32[256,128,128]{2,1,0:T(8,128)} fusion(f32[256,128,128]{2,1,0:T(8,128)} %get-tuple-element.133, s32[64]{0:T(128)S(1)} %get-tuple-element.119, f32[64,128,128]{2,1,0:T(8,128)} %convolution_select_fusion.2), kind=kCustom, calls=%fused_computation.1.clone.1 | custom fusion | flops 1048576 | bytes 12583168 | tf_op jit(solution)/shard_map/while/body/scatter-add | solution.py:62
  134.1 0.7 add_compare_fusion.2
  134.8 0.1 fusion.39
  134.9 3.1 gather_fusion
  138.0 4.3 convolution_select_fusion.2
  142.3 13.7 %scatter_fusion = f32[256,128,128]{2,1,0:T(8,128)} fusion(f32[256,128,128]{2,1,0:T(8,128)} %get-tuple-element.133, s32[64]{0:T(128)S(1)} %get-tuple-element.119, f32[64,128,128]{2,1,0:T(8,128)} %convolution_select_fusion.2), kind=kCustom, calls=%fused_computation.1.clone.1 | custom fusion | flops 1048576 | bytes 12583168 | tf_op jit(solution)/shard_map/while/body/scatter-add | solution.py:62
  155.9 9.2 %convert_element_type.18 = bf16[256,128,128]{2,1,0:T(8,128)(2,1)} convert(f32[256,128,128]{2,1,0:T(8,128)} %get-tuple-element.43) | non-fusion elementwise | flops 4194304 | bytes 25165824 | tf_op jit(solution)/shard_map/convert_element_type | solution.py:70
  165.1 0.0 copy-start.5
  165.1 0.0 reduce-scatter.2.cloned.1.call-update
  165.2 259.5 %reduce-scatter.2.cloned.1.call-done = bf16[2048,128]{1,0:T(8,128)(2,1)} async-done(((bf16[32768,128]{1,0:T(8,128)(2,1)}), bf16[2048,128]{1,0:T(8,128)(2,1)}) %reduce-scatter.2.cloned.1.call-update) | async-done | bytes 524304 | tf_op jit(solution)/shard_map/reduce_scatter | solution.py:69
  424.7 0.0 copy-done
  424.7 0.0 copy-done.5
  424.7 2.4 fusion.7
  (10 shorter events, 0.1 us)
Async XLA Ops:
  6.5 418.2 %copy-start = (bf16[128,256]{1,0:T(8,128)(2,1)S(1)}, bf16[128,256]{1,0:T(8,128)(2,1)}, u32[]{:S(2)}) copy-start(bf16[128,256]{1,0:T(8,128)(2,1)} %param.14) | copy-start | bytes 196612
  6.5 2.3 copy-start.4
  6.5 2.4 copy-start.2
  6.5 2.5 copy-start.3
  17.9 20.6 %all-to-all-start = ((s32[128,1,32]{2,1,0:T(1,128)}), s32[128,1,32]{2,1,0:T(1,128)S(1)}, u32[]{:S(2)}, u32[]{:S(2)}) async-start(s32[128,1,32]{2,1,0:T(1,128)} %copy.15), calls=%async_computation | async-start | bytes 131072 | tf_op jit(solution)/shard_map/all_to_all | solution.py:35
  38.5 26.5 %all-to-all-start.1 = ((bf16[128,32,128]{2,1,0:T(8,128)(2,1)}), bf16[128,32,128]{2,1,0:T(8,128)(2,1)S(1)}, u32[]{:S(2)}, u32[]{:S(2)}) async-start(bf16[128,32,128]{2,1,0:T(8,128)(2,1)} %bitcast.17), calls=%async_computation.1 | async-start | bytes 2097152 | tf_op jit(solution)/shard_map/all_to_all | solution.py:34
  46.0 58.4 %all-gather.2.cloned.1.call-start = ((), (), s32[]{:S(2)}) async-start(), calls=%async_computation.3 | async-start | bytes 4718592 | tf_op jit(solution)/shard_map/all_gather | solution.py:42
  76.6 348.1 %reduce-scatter.2.cloned.1.call-start = ((), (), s32[]{:S(2)}) async-start(), calls=%async_computation.4 | async-start | bytes 8912896 | tf_op jit(solution)/shard_map/reduce_scatter | solution.py:69
  104.4 7.9 %copy-start.1 = (s32[1,1,2,640]{3,2,1,0:T(2,128)S(1)}, s32[1,1,2,640]{3,2,1,0:T(2,128)}, u32[]{:S(2)}) copy-start(s32[1,1,2,640]{3,2,1,0:T(2,128)} %param.12) | copy-start | bytes 15364
  165.1 259.6 %copy-start.5 = (f32[256]{0:T(256)S(1)}, f32[256]{0:T(256)}, u32[]{:S(2)}) copy-start(f32[256]{0:T(256)} %param.15) | copy-start | bytes 3076
Sparse Core Ops, SparseCore 0:
  76.8 27.5 all-gather.1
  165.3 259.3 reduce-scatter.1
where the time goes:
time: 436 us; the launch traced here: 434 us
  waiting for transfers between devices  306 us (70%)
  local copies, waits for them, and re-layouts  42.8 us (10%)
  other arithmetic  41 us (9%)
  starting transfers between devices  18.7 us (4%)
  between operations  14.2 us (3%)
  matrix products  11 us (3%)
    reduce_scatter x1, waiting for transfers between devices, body(): lax.psum_scatter(partial_rows.astype(jnp.bfloat16), 'col', scatter_dimens...  260 us
    scatter-add x2, other arithmetic, add_tiles(): return totals.at[part_rows].add(products)  27.4 us
    all_gather x1, waiting for transfers between devices, body(): column_block = lax.all_gather(moved_rows, 'row', axis=0, tiled=True)  27 us
    all_to_all x1, waiting for transfers between devices, body(): lax.all_to_all(outgoing, ('row', 'col'), split_axis=0, concat_axis=0, til...  17.4 us
    unnamed x14, local copies, waits for them, and re-layouts  15.2 us
    scatter x1, local copies, waits for them, and re-layouts, body(): moved_rows = jnp.zeros((local_rows, feature_width), jnp.bfloat16).at[slot...  11.6 us
    all_to_all x1, starting transfers between devices, body(): lax.all_to_all(slots_out, ('row', 'col'), split_axis=0, concat_axis=0, ti...  11.1 us
    convert_element_type x1, other arithmetic, body(): partial_rows.astype(jnp.bfloat16)  9.2 us
  transfers between devices with their start and end apart: 4, of which 4 were waited for; matrix products, arithmetic and copies ran while one was open for 2% of the time, Pallas kernels for 0%

commit v1 on v0

--- a/solution.py
+++ b/solution.py
@@ -39,7 +39,12 @@
         .at[slots_in.reshape(-1)]
         .set(rows_in.reshape(-1, feature_width), mode="drop")
     )
-    column_block = lax.all_gather(moved_rows, "row", axis=0, tiled=True)
+    ring = [moved_rows]
+    for hop in range(7):
+        ring.append(lax.ppermute(ring[-1], "row", [(dev, (dev + 1) % 8) for dev in range(8)]))
+    column_block = jnp.roll(
+        jnp.concatenate(ring[::-1], axis=0), (lax.axis_index("row") + 1) * ring[0].shape[0], axis=0
+    )
     tile_set = tile_values[0, 0]
     tile_coords = tile_index[0, 0]
     tile_total = tile_count[0, 0]

time: 436 us -> 481 us (1.10)
  waiting for transfers between devices: 306 us -> 343 us
  local copies, waits for them, and re-layouts: 42.8 us -> 49.5 us
    ppermute x0 -> x7, waiting for transfers between devices: none -> 68.4 us  [body(): lax.ppermute(ring[-1], 'row', [(dev, (dev + 1) % 8) for dev in range(8)])]
    all_gather x1 -> x0, waiting for transfers between devices: 27 us -> none  [body(): column_block = lax.all_gather(moved_rows, 'row', axis=0, tiled=True)]
    reduce_scatter x1, waiting for transfers between devices: 260 us -> 254 us  [body(): lax.psum_scatter(partial_rows.astype(jnp.bfloat16), 'col', scatter_dimens...]
    unnamed x14 -> x23, local copies, waits for them, and re-layouts: 15.2 us -> 20.4 us
  transfers between devices with their start and end apart: 4 -> 10, of which waited for: 4 -> 10; matrix products, arithmetic and copies ran while one was open for 2% -> 2% of each run, Pallas kernels for 0% -> 0%
where the time goes in v1:
time: 481 us; the launch traced here: 478 us
  waiting for transfers between devices  343 us (71%)
  local copies, waits for them, and re-layouts  49.5 us (10%)
  other arithmetic  42.3 us (9%)
  starting transfers between devices  18.7 us (4%)
  between operations  14.3 us (3%)
  matrix products  11 us (2%)
    reduce_scatter x1, waiting for transfers between devices, body(): lax.psum_scatter(partial_rows.astype(jnp.bfloat16), 'col', scatter_dimens...  254 us
    ppermute x7, waiting for transfers between devices, body(): lax.ppermute(ring[-1], 'row', [(dev, (dev + 1) % 8) for dev in range(8)])  68.4 us
    scatter-add x2, other arithmetic, add_tiles(): return totals.at[part_rows].add(products)  27.4 us
    unnamed x23, local copies, waits for them, and re-layouts  20.4 us
    all_to_all x1, waiting for transfers between devices, body(): lax.all_to_all(outgoing, ('row', 'col'), split_axis=0, concat_axis=0, til...  17.4 us
    all_to_all x1, starting transfers between devices, body(): lax.all_to_all(slots_out, ('row', 'col'), split_axis=0, concat_axis=0, ti...  11.1 us
    scatter x1, local copies, waits for them, and re-layouts, body(): moved_rows = jnp.zeros((local_rows, feature_width), jnp.bfloat16).at[slot...  10.9 us
  transfers between devices with their start and end apart: 10, of which 10 were waited for; matrix products, arithmetic and copies ran while one was open for 2% of the time, Pallas kernels for 0%

profile of v1, /device:TPU:0, one launch (start us, length us, event | category | flops | bytes accessed | tf_op | source)
XLA Modules:
  0.0 478.3 jit_solution(16111796767804228149)
XLA Ops:
  6.5 0.8 compare_select_fusion.4
  7.3 0.1 copy.13
  7.4 0.3 fusion.10
  7.8 0.1 broadcast_add_fusion
  7.9 0.3 copy.14
  8.2 0.6 fusion.9
  8.9 0.8 and_reduce_fusion
  9.6 0.8 multiply_reduce_fusion
  10.4 8.1 %scatter_custom_fusion.2 = s32[4096]{0:T(1024)S(1)} fusion(s32[2048]{0:T(1024)S(1)} %get-tuple-element.68, s32[2048]{0:T(1024)S(1)} %get-tuple-element.66, s32[]{:T(128)} %constant.115.clone.1), kind=kCustom, calls=%fused_computation.70 | custom fusion | bytes 16388
  18.5 0.7 copy.15
  19.2 11.1 %all-to-all-start = ((s32[128,1,32]{2,1,0:T(1,128)}), s32[128,1,32]{2,1,0:T(1,128)S(1)}, u32[]{:S(2)}, u32[]{:S(2)}) async-start(s32[128,1,32]{2,1,0:T(1,128)} %copy.15), calls=%async_computation | async-start | bytes 131072 | tf_op jit(solution)/shard_map/all_to_all | solution.py:35
  30.4 7.1 %scatter_custom_fusion.3 = bf16[4096,128]{1,0:T(8,128)(2,1)} fusion(s32[2048]{0:T(1024)S(1)} %get-tuple-element.67, bf16[2048,128]{1,0:T(8,128)(2,1)} %param.9, bf16[]{:T(256)} %constant.114.clone.1), kind=kCustom, calls=%fused_computation.28 | custom fusion | bytes 1049088
  37.5 2.3 all-to-all-done
  39.8 7.4 %all-to-all-start.1 = ((bf16[128,32,128]{2,1,0:T(8,128)(2,1)}), bf16[128,32,128]{2,1,0:T(8,128)(2,1)S(1)}, u32[]{:S(2)}, u32[]{:S(2)}) async-start(bf16[128,32,128]{2,1,0:T(8,128)(2,1)} %bitcast.17), calls=%async_computation.1 | async-start | bytes 2097152 | tf_op jit(solution)/shard_map/all_to_all | solution.py:34
  47.3 0.0 reduce-scatter.2.cloned.1.call-start
  47.3 0.6 broadcast.175
  47.9 0.8 reduce.10
  48.8 0.1 reshape.136
  48.9 17.4 %all-to-all-done.1 = bf16[128,32,128]{2,1,0:T(8,128)(2,1)S(1)} async-done(((bf16[128,32,128]{2,1,0:T(8,128)(2,1)}), bf16[128,32,128]{2,1,0:T(8,128)(2,1)S(1)}, u32[]{:S(2)}, u32[]{:S(2)}) %all-to-all-start.1) | async-done | bytes 1048608 | tf_op jit(solution)/shard_map/all_to_all | solution.py:34
  66.3 10.9 %scatter_custom_fusion.1 = bf16[2048,128]{1,0:T(8,128)(2,1)S(1)} fusion(s32[4096]{0:T(1024)S(1)} %bitcast.65, bf16[4096,128]{1,0:T(8,128)(2,1)S(1)} %bitcast.58, bf16[]{:T(256)} %constant.114.clone.1), kind=kCustom, calls=%fused_computation.32 | custom fusion | bytes 524290 | tf_op jit(solution)/shard_map/scatter | solution.py:40
  77.3 0.0 collective-permute-start
  77.3 9.8 %collective-permute-done = bf16[2048,128]{1,0:T(8,128)(2,1)S(1)} collective-permute-done((bf16[2048,128]{1,0:T(8,128)(2,1)S(1)}, bf16[2048,128]{1,0:T(8,128)(2,1)S(1)}, u32[]{:S(2)}, u32[]{:S(2)}) %collective-permute-start) | collective-permute-done | bytes 524320 | tf_op jit(solution)/shard_map/ppermute | solution.py:44
  87.1 9.8 %collective-permute-done.1 = bf16[2048,128]{1,0:T(8,128)(2,1)S(1)} collective-permute-done((bf16[2048,128]{1,0:T(8,128)(2,1)S(1)}, bf16[2048,128]{1,0:T(8,128)(2,1)S(1)}, u32[]{:S(2)}, u32[]{:S(2)}) %collective-permute-start.1) | collective-permute-done | bytes 524320 | tf_op jit(solution)/shard_map/ppermute | solution.py:44
  96.9 0.0 collective-permute-start.2
  96.9 9.8 %collective-permute-done.2 = bf16[2048,128]{1,0:T(8,128)(2,1)S(1)} collective-permute-done((bf16[2048,128]{1,0:T(8,128)(2,1)S(1)}, bf16[2048,128]{1,0:T(8,128)(2,1)S(1)}, u32[]{:S(2)}, u32[]{:S(2)}) %collective-permute-start.2) | collective-permute-done | bytes 524320 | tf_op jit(solution)/shard_map/ppermute | solution.py:44
  106.7 0.0 collective-permute-start.3
  106.7 9.8 %collective-permute-done.3 = bf16[2048,128]{1,0:T(8,128)(2,1)S(1)} collective-permute-done((bf16[2048,128]{1,0:T(8,128)(2,1)S(1)}, bf16[2048,128]{1,0:T(8,128)(2,1)S(1)}, u32[]{:S(2)}, u32[]{:S(2)}) %collective-permute-start.3) | collective-permute-done | bytes 524320 | tf_op jit(solution)/shard_map/ppermute | solution.py:44
  116.5 9.8 %collective-permute-done.4 = bf16[2048,128]{1,0:T(8,128)(2,1)S(1)} collective-permute-done((bf16[2048,128]{1,0:T(8,128)(2,1)S(1)}, bf16[2048,128]{1,0:T(8,128)(2,1)S(1)}, u32[]{:S(2)}, u32[]{:S(2)}) %collective-permute-start.4) | collective-permute-done | bytes 524320 | tf_op jit(solution)/shard_map/ppermute | solution.py:44
  126.4 0.0 collective-permute-start.5
  126.4 9.9 %collective-permute-done.5 = bf16[2048,128]{1,0:T(8,128)(2,1)} collective-permute-done((bf16[2048,128]{1,0:T(8,128)(2,1)S(1)}, bf16[2048,128]{1,0:T(8,128)(2,1)}, u32[]{:S(2)}, u32[]{:S(2)}) %collective-permute-start.5) | collective-permute-done | bytes 524320 | tf_op jit(solution)/shard_map/ppermute | solution.py:44
  137.0 9.4 %collective-permute-done.6 = bf16[2048,128]{1,0:T(8,128)(2,1)} collective-permute-done((bf16[2048,128]{1,0:T(8,128)(2,1)}, bf16[2048,128]{1,0:T(8,128)(2,1)}, u32[]{:S(2)}, u32[]{:S(2)}) %collective-permute-start.6) | collective-permute-done | bytes 524320 | tf_op jit(solution)/shard_map/ppermute | solution.py:44
  146.4 1.1 constant_dynamic-update-slice_fusion.15
  147.5 1.1 constant_dynamic-update-slice_fusion.14
  148.6 0.1 constant_dynamic-update-slice_fusion.13
  148.7 0.1 constant_dynamic-update-slice_fusion.12
  148.8 0.1 constant_dynamic-update-slice_fusion.11
  148.8 0.1 constant_dynamic-update-slice_fusion.10
  148.9 0.1 constant_dynamic-update-slice_fusion.9
  149.0 0.1 constant_dynamic-update-slice_fusion.8
  149.1 1.1 constant_dynamic-update-slice_fusion.7
  150.2 1.1 constant_dynamic-update-slice_fusion.6
  151.3 0.1 constant_dynamic-update-slice_fusion.5
  151.4 0.1 constant_dynamic-update-slice_fusion.4
  151.5 0.1 constant_dynamic-update-slice_fusion.3
  151.5 0.1 constant_dynamic-update-slice_fusion.2
  151.6 0.1 constant_dynamic-update-slice_fusion.1
  151.7 0.1 constant_dynamic-update-slice_fusion
  151.8 2.1 constant_dynamic-slice_fusion.2
  153.9 7.8 %broadcast_in_dim.15 = f32[256,128,128]{2,1,0:T(8,128)} broadcast(f32[]{:T(128)} %constant.109.clone.1), dimensions={} | broadcast | bytes 16777220 | tf_op jit(solution)/shard_map/broadcast_in_dim | solution.py:71
  161.7 43.7 %while.10 = (s32[]{:T(128)}, f32[256,128,128]{2,1,0:T(8,128)}, s32[]{:T(128)}, s32[2,640]{1,0:T(2,128)S(1)}, s32[]{:T(128)}, /*index=5*/bf16[640,128,128]{2,1,0:...) while((s32[]{:T(128)}, f32[256,128,128]{2,1,0:T(8,128)}, ...), condition=%wide.region_8.9_spmd, body=%wide.region_6.8_spmd.sunk | while | flops 270534144 | bytes 25182252 | solution.py:70
  161.7 0.7 add_compare_fusion.2
  162.4 0.1 fusion.39
  162.5 3.1 gather_fusion
  165.6 4.3 convolution_select_fusion.2
  169.9 13.7 %scatter_fusion = f32[256,128,128]{2,1,0:T(8,128)} fusion(f32[256,128,128]{2,1,0:T(8,128)} %get-tuple-element.133, s32[64]{0:T(128)S(1)} %get-tuple-element.119, f32[64,128,128]{2,1,0:T(8,128)} %convolution_select_fusion.2), kind=kCustom, calls=%fused_computation.1.clone.1 | custom fusion | flops 1048576 | bytes 12583168 | tf_op jit(solution)/shard_map/while/body/scatter-add | solution.py:67
  183.6 0.7 add_compare_fusion.2
  184.3 0.1 fusion.39
  184.3 3.1 gather_fusion
  187.5 4.3 convolution_select_fusion.2
  191.8 13.7 %scatter_fusion = f32[256,128,128]{2,1,0:T(8,128)} fusion(f32[256,128,128]{2,1,0:T(8,128)} %get-tuple-element.133, s32[64]{0:T(128)S(1)} %get-tuple-element.119, f32[64,128,128]{2,1,0:T(8,128)} %convolution_select_fusion.2), kind=kCustom, calls=%fused_computation.1.clone.1 | custom fusion | flops 1048576 | bytes 12583168 | tf_op jit(solution)/shard_map/while/body/scatter-add | solution.py:67
  205.4 9.2 %convert_element_type.18 = bf16[256,128,128]{2,1,0:T(8,128)(2,1)} convert(f32[256,128,128]{2,1,0:T(8,128)} %get-tuple-element.43) | non-fusion elementwise | flops 4194304 | bytes 25165824 | tf_op jit(solution)/shard_map/convert_element_type | solution.py:75
  214.6 0.0 reduce-scatter.2.cloned.1.call-update
  214.7 254.3 %reduce-scatter.2.cloned.1.call-done = bf16[2048,128]{1,0:T(8,128)(2,1)} async-done(((bf16[32768,128]{1,0:T(8,128)(2,1)}), bf16[2048,128]{1,0:T(8,128)(2,1)}) %reduce-scatter.2.cloned.1.call-update) | async-done | bytes 524304 | tf_op jit(solution)/shard_map/reduce_scatter | solution.py:74
  469.0 2.4 fusion.7
  (19 shorter events, 0.1 us)
Async XLA Ops:
  6.5 462.4 %copy-start = (bf16[128,256]{1,0:T(8,128)(2,1)S(1)}, bf16[128,256]{1,0:T(8,128)(2,1)}, u32[]{:S(2)}) copy-start(bf16[128,256]{1,0:T(8,128)(2,1)} %param.14) | copy-start | bytes 196612
  19.2 20.6 %all-to-all-start = ((s32[128,1,32]{2,1,0:T(1,128)}), s32[128,1,32]{2,1,0:T(1,128)S(1)}, u32[]{:S(2)}, u32[]{:S(2)}) async-start(s32[128,1,32]{2,1,0:T(1,128)} %copy.15), calls=%async_computation | async-start | bytes 131072 | tf_op jit(solution)/shard_map/all_to_all | solution.py:35
  39.8 26.5 %all-to-all-start.1 = ((bf16[128,32,128]{2,1,0:T(8,128)(2,1)}), bf16[128,32,128]{2,1,0:T(8,128)(2,1)S(1)}, u32[]{:S(2)}, u32[]{:S(2)}) async-start(bf16[128,32,128]{2,1,0:T(8,128)(2,1)} %bitcast.17), calls=%async_computation.1 | async-start | bytes 2097152 | tf_op jit(solution)/shard_map/all_to_all | solution.py:34
  47.3 421.7 %reduce-scatter.2.cloned.1.call-start = ((), (), s32[]{:S(2)}) async-start(), calls=%async_computation.3 | async-start | bytes 8912896 | tf_op jit(solution)/shard_map/reduce_scatter | solution.py:74
  77.3 9.8 %collective-permute-start = (bf16[2048,128]{1,0:T(8,128)(2,1)S(1)}, bf16[2048,128]{1,0:T(8,128)(2,1)S(1)}, u32[]{:S(2)}, u32[]{:S(2)}) collective-permute-start(bf16[2048,128]{1,0:T(8,128)(2,1)S(1)} %scatter_custom_fusion.1), channel_id=1, source_target_pairs={{0,16},{16,32},{32,48},{48,64},{64,80},{80,96},{96,112},{112,0},{1... | collective-permute-start | bytes 1572872 | tf_op jit(solution)/shard_map/ppermute | solution.py:44
  87.1 9.8 %collective-permute-start.1 = (bf16[2048,128]{1,0:T(8,128)(2,1)S(1)}, bf16[2048,128]{1,0:T(8,128)(2,1)S(1)}, u32[]{:S(2)}, u32[]{:S(2)}) collective-permute-start(bf16[2048,128]{1,0:T(8,128)(2,1)S(1)} %collective-permute-done), channel_id=1, source_target_pairs={{0,16},{16,32},{32,48},{48,64},{64,80},{80,96},{96,112},{112,0},{1... | collective-permute-start | bytes 1572872 | tf_op jit(solution)/shard_map/ppermute | solution.py:44
  96.9 9.8 %collective-permute-start.2 = (bf16[2048,128]{1,0:T(8,128)(2,1)S(1)}, bf16[2048,128]{1,0:T(8,128)(2,1)S(1)}, u32[]{:S(2)}, u32[]{:S(2)}) collective-permute-start(bf16[2048,128]{1,0:T(8,128)(2,1)S(1)} %collective-permute-done.1), channel_id=1, source_target_pairs={{0,16},{16,32},{32,48},{48,64},{64,80},{80,96},{96,112},{112,0},{1... | collective-permute-start | bytes 1572872 | tf_op jit(solution)/shard_map/ppermute | solution.py:44
  106.7 9.8 %collective-permute-start.3 = (bf16[2048,128]{1,0:T(8,128)(2,1)S(1)}, bf16[2048,128]{1,0:T(8,128)(2,1)S(1)}, u32[]{:S(2)}, u32[]{:S(2)}) collective-permute-start(bf16[2048,128]{1,0:T(8,128)(2,1)S(1)} %collective-permute-done.2), channel_id=1, source_target_pairs={{0,16},{16,32},{32,48},{48,64},{64,80},{80,96},{96,112},{112,0},{1... | collective-permute-start | bytes 1572872 | tf_op jit(solution)/shard_map/ppermute | solution.py:44
  116.5 9.8 %collective-permute-start.4 = (bf16[2048,128]{1,0:T(8,128)(2,1)S(1)}, bf16[2048,128]{1,0:T(8,128)(2,1)S(1)}, u32[]{:S(2)}, u32[]{:S(2)}) collective-permute-start(bf16[2048,128]{1,0:T(8,128)(2,1)S(1)} %collective-permute-done.3), channel_id=1, source_target_pairs={{0,16},{16,32},{32,48},{48,64},{64,80},{80,96},{96,112},{112,0},{1... | collective-permute-start | bytes 1572872 | tf_op jit(solution)/shard_map/ppermute | solution.py:44
  126.4 9.9 %collective-permute-start.5 = (bf16[2048,128]{1,0:T(8,128)(2,1)S(1)}, bf16[2048,128]{1,0:T(8,128)(2,1)}, u32[]{:S(2)}, u32[]{:S(2)}) collective-permute-start(bf16[2048,128]{1,0:T(8,128)(2,1)S(1)} %collective-permute-done.4), channel_id=1, source_target_pairs={{0,16},{16,32},{32,48},{48,64},{64,80},{80,96},{96,112},{112,0},{1... | collective-permute-start | bytes 1572872 | tf_op jit(solution)/shard_map/ppermute | solution.py:44
  136.3 10.1 %collective-permute-start.6 = (bf16[2048,128]{1,0:T(8,128)(2,1)}, bf16[2048,128]{1,0:T(8,128)(2,1)}, u32[]{:S(2)}, u32[]{:S(2)}) collective-permute-start(bf16[2048,128]{1,0:T(8,128)(2,1)} %collective-permute-done.5), channel_id=1, source_target_pairs={{0,16},{16,32},{32,48},{48,64},{64,80},{80,96},{96,112},{112,0},{1... | collective-permute-start | bytes 1572872 | tf_op jit(solution)/shard_map/ppermute | solution.py:44
  153.9 7.9 %copy-start.1 = (s32[1,1,2,640]{3,2,1,0:T(2,128)S(1)}, s32[1,1,2,640]{3,2,1,0:T(2,128)}, u32[]{:S(2)}) copy-start(s32[1,1,2,640]{3,2,1,0:T(2,128)} %param.12) | copy-start | bytes 15364
  214.6 254.3 %copy-start.2 = (f32[256]{0:T(256)S(1)}, f32[256]{0:T(256)}, u32[]{:S(2)}) copy-start(f32[256]{0:T(256)} %param.15) | copy-start | bytes 3076
Sparse Core Ops, SparseCore 0:
  214.8 254.1 reduce-scatter.1
